TPU v7x, 512 devices: a whole 4x8x8 slice. The times are simulated.
512 devices in a mesh: dp: 64 (over x, z_lo, y), ctx: 8 (over z_hi, core).
Axes of the slice: x: 4, y: 8, z: 8 (z_hi: 4, z_lo: 2; z = z_hi * 2 + z_lo), core: 2. Of those that a mesh axis runs over, the one named last changes fastest.
Arguments:
- queries: bfloat16 [65536, 4096], P(('dp', 'ctx')), may hold values from -150 to 150
- keys: bfloat16 [65536, 512], P(('dp', 'ctx')), may hold values from -4 to 4
- values: bfloat16 [65536, 512], P(('dp', 'ctx')), may hold values from -6 to 6
- lengths: int32 [128], replicated, may hold values from 1 to 2048, 65536 in all
Outputs:
- attended: bfloat16 [65536, 4096], P(('dp', 'ctx'))
Inputs may be any that keep to these rules, and one draw needn't show every extreme that they name: lengths of the 128 documents sum to 65536; the largest is exactly 2048.
All inputs are finite; a program needn't handle non-finite values.
Results may differ from a plain program's by a relative error of at most 0.0045.
Values may be sent and summed in bfloat16 or wider, within the bound.
A program may use at most 128 MiB of HBM per device.

v0:
```python
import functools
import math

import jax
import jax.numpy as jnp
from jax import lax
from jax.experimental import pallas as pl
from jax.experimental.pallas import tpu as pltpu
from jax.sharding import PartitionSpec as P

HEAD_SIZE = 128
QUERY_HEADS = 32
KEY_VALUE_HEADS = 4
GROUP = QUERY_HEADS // KEY_VALUE_HEADS
BLOCK = 128
SLOTS = 9
STACK = 2
NEG = -1e30
EXPONENT_SCALE = math.log2(math.e) / math.sqrt(HEAD_SIZE)
MESH = pl.DeviceIdType.MESH


def kernel(
    dp_size, columns,
    q_hbm, k_hbm, v_hbm, len_ref, out_ref,
    window, q_ref, hot_ref, qmask_ref, max_ref, acc_ref,
    load_sem, recv_sem, pair_recv_sem, row_send_sem, column_send_sem, pair_send_sem,
):
    row = lax.axis_index("dp")
    ctx = lax.axis_index("ctx")
    column, core = ctx // 2, ctx % 2
    chip = row * columns + column
    next_row, last_row = (row + 1) % dp_size, (row + dp_size - 1) % dp_size
    pair = (row, column * 2 + 1 - core)

    def in_row(step):
        return (row, ((column + step) % columns) * 2 + core)

    load_k = pltpu.make_async_copy(k_hbm, window.at[0, core, 0], load_sem.at[0])
    load_v = pltpu.make_async_copy(v_hbm, window.at[0, core, 1], load_sem.at[1])
    load_q = pltpu.make_async_copy(q_hbm, q_ref, load_sem.at[2])
    load_k.start()
    load_v.start()
    load_q.start()

    barrier = pltpu.get_barrier_semaphore()
    partners = [in_row(step) for step in range(1, columns)]
    partners += [(next_row, ctx), (last_row, ctx), pair]
    for partner in partners:
        pl.semaphore_signal(barrier, inc=1, device_id=partner, device_id_type=MESH)
    pl.semaphore_wait(barrier, len(partners))

    def along_rows(slot):
        return pltpu.make_async_remote_copy(
            src_ref=window.at[slot, core],
            dst_ref=window.at[slot + columns, core],
            send_sem=row_send_sem.at[slot],
            recv_sem=recv_sem.at[slot + columns],
            device_id=(next_row, ctx),
            device_id_type=MESH,
        )

    def along_columns(step):
        source = jnp.where(column + step < columns, 0, columns)
        return pltpu.make_async_remote_copy(
            src_ref=window.at[source, core],
            dst_ref=window.at[step, core],
            send_sem=column_send_sem.at[step],
            recv_sem=recv_sem.at[step],
            device_id=in_row(step),
            device_id_type=MESH,
        )

    def to_pair(slot):
        return pltpu.make_async_remote_copy(
            src_ref=window.at[slot, core],
            dst_ref=window.at[slot, core],
            send_sem=pair_send_sem.at[slot],
            recv_sem=pair_recv_sem.at[slot],
            device_id=pair,
            device_id_type=MESH,
        )

    def arrived(slot):
        pltpu.make_async_copy(
            window.at[slot, core], window.at[slot, core], recv_sem.at[slot]
        ).wait()

    def pair_arrived(slot):
        pltpu.make_async_copy(
            window.at[slot, 1 - core], window.at[slot, 1 - core], pair_recv_sem.at[slot]
        ).wait()

    load_k.wait()
    load_v.wait()
    along_rows(0).start()
    for step in range(1, columns):
        @pl.when(column + step < columns)
        def _():
            along_columns(step).start()
    to_pair(0).start()

    lengths = len_ref[...].astype(jnp.float32)
    ndocs = lengths.shape[1]
    sub = lax.broadcasted_iota(jnp.int32, (ndocs, ndocs), 0)
    lane = lax.broadcasted_iota(jnp.int32, (ndocs, ndocs), 1)
    as_column = jnp.sum(jnp.where(sub == lane, lengths, 0.0), axis=1, keepdims=True)
    ends = jnp.sum(jnp.where(sub <= lane, as_column, 0.0), axis=0, keepdims=True)
    begins = ends - lengths
    ends = ends.astype(jnp.int32)
    begins = begins.astype(jnp.int32)
    query_pos = (chip * 2 + core) * BLOCK + lax.broadcasted_iota(jnp.int32, (BLOCK, ndocs), 0)
    same = (query_pos >= begins) & (query_pos < ends)
    qmask_ref[...] = jnp.where(same, 0.0, NEG).astype(jnp.bfloat16)

    @pl.loop(0, SLOTS)
    def _(slot):
        key_pos = (chip - slot) * (2 * BLOCK) + lax.broadcasted_iota(
            jnp.int32, (2 * BLOCK, ndocs), 0
        )
        inside = ((key_pos >= begins) & (key_pos < ends)) | (key_pos < 0)
        hot_ref[slot] = jnp.where(inside, 1.0, 0.0).astype(jnp.bfloat16)

    load_q.wait()

    def attend(slots, first, last):
        count = 2 * BLOCK * len(slots)

        @pl.loop(0, KEY_VALUE_HEADS)
        def _(head):
            lanes = pl.ds(pl.multiple_of(head * HEAD_SIZE, HEAD_SIZE), HEAD_SIZE)
            key = jnp.concatenate([window[s, p, 0, :, lanes] for s in slots for p in (0, 1)], axis=0)
            hot = jnp.concatenate([hot_ref[s] for s in slots], axis=0)
            key = jnp.concatenate([key, hot], axis=1)
            value = jnp.concatenate([window[s, p, 1, :, lanes] for s in slots for p in (0, 1)], axis=0)
            value = jnp.concatenate([value, jnp.ones((count, HEAD_SIZE), jnp.bfloat16)], axis=1)
            for inner in range(0, GROUP, STACK):
                heads = [head * GROUP + inner + i for i in range(STACK)]
                spans = [
                    pl.ds(pl.multiple_of(n * HEAD_SIZE, HEAD_SIZE), HEAD_SIZE) for n in heads
                ]
                query = jnp.concatenate([q_ref[:, span] for span in spans], axis=0)
                mask = jnp.concatenate([qmask_ref[...]] * STACK, axis=0)
                query = jnp.concatenate([query, mask], axis=1)
                scores = lax.dot_general(
                    query, key, (((1,), (1,)), ((), ())), preferred_element_type=jnp.float32
                )
                rows = pl.ds(
                    pl.multiple_of(heads[0] * BLOCK, STACK * BLOCK), STACK * BLOCK
                )
                if first:
                    key_at = lax.broadcasted_iota(jnp.int32, scores.shape, 1)
                    query_at = lax.broadcasted_iota(jnp.int32, scores.shape, 0) % BLOCK
                    scores = jnp.where(key_at <= query_at + core * BLOCK, scores, NEG)
                top = jnp.max(scores, axis=1, keepdims=True)
                if first:
                    top = jnp.broadcast_to(top, (STACK * BLOCK, HEAD_SIZE))
                else:
                    old = max_ref[rows, :]
                    top = jnp.maximum(old, top)
                wide = jnp.concatenate([top] * (count // HEAD_SIZE), axis=1)
                weights = jnp.exp2((scores - wide) * EXPONENT_SCALE).astype(jnp.bfloat16)
                total = jnp.dot(weights, value, preferred_element_type=jnp.float32)
                if not first:
                    rescale = jnp.exp2((old - top) * EXPONENT_SCALE)
                    total = acc_ref[rows, :] * jnp.concatenate([rescale] * 2, axis=1) + total
                if last:
                    result = (total[:, :HEAD_SIZE] / total[:, HEAD_SIZE:]).astype(jnp.bfloat16)
                    for i, span in enumerate(spans):
                        out_ref[:, span] = result[i * BLOCK:(i + 1) * BLOCK, :]
                else:
                    acc_ref[rows, :] = total
                    max_ref[rows, :] = top

    pair_arrived(0)
    attend([0], True, False)

    arrived(columns)
    for step in range(1, columns):
        @pl.when(column + step >= columns)
        def _():
            along_columns(step).start()
    along_rows(columns).start()
    to_pair(columns).start()
    for slot in range(1, columns):
        arrived(slot)
        along_rows(slot).start()
        to_pair(slot).start()

    def middle(turn, carry):
        one, two = 2 * turn + 1, 2 * turn + 2

        @pl.when(turn == 2)
        def _():
            for slot in (one, two):
                arrived(slot)
                to_pair(slot).start()

        pair_arrived(one)
        pair_arrived(two)
        attend([one, two], False, False)
        return carry

    lax.fori_loop(0, 3, middle, 0)
    for slot in (7, 8):
        arrived(slot)
        to_pair(slot).start()
    pair_arrived(7)
    pair_arrived(8)
    attend([7, 8], False, True)

    for slot in range(columns + 1):
        along_rows(slot).wait_send()
    for step in range(1, columns):
        along_columns(step).wait_send()
    for slot in range(SLOTS):
        to_pair(slot).wait_send()


def per_device(queries, keys, values, lengths):
    columns = lax.axis_size("ctx") // 2
    dp_size = lax.axis_size("dp")
    rows = queries.shape[0]
    kv_width = keys.shape[1]
    ndocs = lengths.shape[0]
    any_space = pl.BlockSpec(memory_space=pl.ANY)
    vmem = pl.BlockSpec(memory_space=pltpu.VMEM)
    flops = 4 * rows * QUERY_HEADS * SLOTS * 2 * BLOCK * 2 * HEAD_SIZE
    return pl.pallas_call(
        functools.partial(kernel, dp_size, columns),
        out_shape=jax.ShapeDtypeStruct(queries.shape, jnp.bfloat16),
        in_specs=[any_space, any_space, any_space, vmem],
        out_specs=vmem,
        scratch_shapes=[
            pltpu.VMEM((SLOTS, 2, 2, BLOCK, kv_width), jnp.bfloat16),
            pltpu.VMEM(queries.shape, jnp.bfloat16),
            pltpu.VMEM((SLOTS, 2 * BLOCK, ndocs), jnp.bfloat16),
            pltpu.VMEM((BLOCK, ndocs), jnp.bfloat16),
            pltpu.VMEM((QUERY_HEADS * BLOCK, HEAD_SIZE), jnp.float32),
            pltpu.VMEM((QUERY_HEADS * BLOCK, 2 * HEAD_SIZE), jnp.float32),
            pltpu.SemaphoreType.DMA((3,)),
            pltpu.SemaphoreType.DMA((SLOTS,)),
            pltpu.SemaphoreType.DMA((SLOTS,)),
            pltpu.SemaphoreType.DMA((SLOTS,)),
            pltpu.SemaphoreType.DMA((columns,)),
            pltpu.SemaphoreType.DMA((SLOTS,)),
        ],
        compiler_params=pltpu.CompilerParams(
            collective_id=0, has_side_effects=True, vmem_limit_bytes=48 * 1024 * 1024
        ),
        cost_estimate=pl.CostEstimate(
            flops=flops, bytes_accessed=4 * queries.size, transcendentals=0
        ),
    )(queries, keys, values, lengths.reshape(1, ndocs))


def solution(mesh):
    in_specs = (P(("dp", "ctx"), None), P(("dp", "ctx"), None), P(("dp", "ctx"), None), P())
    out_specs = P(("dp", "ctx"), None)
    return jax.shard_map(
        per_device, mesh=mesh, in_specs=in_specs, out_specs=out_specs, check_vma=False
    )
```

profile of v0, /device:TPU:1, one launch (start us, length us, event | category | flops | bytes accessed | tf_op | source)
XLA Modules:
  0.0 95.7 jit_solution(10050878407864213403)
XLA Ops:
  0.0 0.0 copy-start.3
  0.0 0.7 copy-done.3
  0.7 0.0 copy-start
  0.7 1.2 %copy-done = bf16[128,4096]{1,0:T(8,128)(2,1)S(1)} copy-done((bf16[128,4096]{1,0:T(8,128)(2,1)S(1)}, bf16[128,4096]{1,0:T(8,128)(2,1)}, u32[]{:S(2)}) %copy-start) | copy-done | bytes 1048600
  1.9 0.0 copy-start.1
  1.9 0.9 copy-done.1
  2.8 0.0 copy-start.2
  2.8 0.9 copy-done.2
  3.7 91.1 %shard_map.46 = bf16[128,4096]{1,0:T(8,128)(2,1)S(1)} custom-call(bf16[128,4096]{1,0:T(8,128)(2,1)S(1)} %copy-done, bf16[128,512]{1,0:T(8,128)(2,1)S(1)} %copy-done.1, bf16[128,512]{1,0:T(8,128)(2,1)S(1)} %copy-done.2, s32[1,128]{1,0:T(1,128)S(1)} %bitcast.1), custom_call_target="tpu_custom_call" | custom-call | flops 9663676416 | bytes 2097152 | tf_op jit(solution)/shard_map/pallas_call | solution.py:229
  94.8 1.0 %copy.6 = bf16[128,4096]{1,0:T(8,128)(2,1)} copy(bf16[128,4096]{1,0:T(8,128)(2,1)S(1)} %shard_map.46) | data formatting | bytes 2097152
Async XLA Ops:
  0.0 0.7 copy-start.3
  0.7 1.2 %copy-start = (bf16[128,4096]{1,0:T(8,128)(2,1)S(1)}, bf16[128,4096]{1,0:T(8,128)(2,1)}, u32[]{:S(2)}) copy-start(bf16[128,4096]{1,0:T(8,128)(2,1)} %q_hbm.1) | copy-start | bytes 3145732
  1.9 0.9 copy-start.1
  2.8 0.9 copy-start.2
where the time goes:
time: 95.9 us; the launch traced here: 95.7 us
  Pallas kernels  91.1 us (95%)
  local copies, waits for them, and re-layouts  4.66 us (5%)
    pallas_call x1, Pallas kernels, per_device(): pl.pallas_call(functools.partial(kernel, dp_size, columns), out_shape=jax...  91.1 us
    unnamed x9, local copies, waits for them, and re-layouts  4.66 us

commit v1 on v0

v1 whole, which is shorter than its diff:
```python
import functools
import math

import jax
import jax.numpy as jnp
from jax import lax
from jax.experimental import pallas as pl
from jax.experimental.pallas import tpu as pltpu
from jax.sharding import PartitionSpec as P

HEAD_SIZE = 128
QUERY_HEADS = 32
KEY_VALUE_HEADS = 4
GROUP = QUERY_HEADS // KEY_VALUE_HEADS
BLOCK = 128
SLOTS = 9
TURN = 8
RELAYED = 2
STACK = 2
DIRECT = KEY_VALUE_HEADS - RELAYED
NEG = -1e30
EXPONENT_SCALE = math.log2(math.e) / math.sqrt(HEAD_SIZE)
MESH = pl.DeviceIdType.MESH


def kernel(
    dp_size, columns, turn,
    q_hbm, k_hbm, v_hbm, len_ref, out_ref,
    window, relay, q_ref, hot_ref, qmask_ref, max_ref, acc_ref,
    load_sem, query_sem, recv_sem, relay_recv_sem, pair_recv_sem, row_send_sem, relay_send_sem, column_send_sem, pair_send_sem,
):
    row = lax.axis_index("dp")
    ctx = lax.axis_index("ctx")
    column, core = ctx // 2, ctx % 2
    chip = row * columns + column
    next_row, last_row = (row + 1) % dp_size, (row + dp_size - 1) % dp_size
    pair = (row, column * 2 + 1 - core)

    def beside(of_row):
        return of_row + turn - 2 * turn * (of_row // turn % 2)

    at_turn = row % turn == turn - 1
    relay_to = (beside(row), ctx)
    relayed_to = ((beside(row) + 1) % dp_size, ctx)
    relayed_from = (beside(last_row), ctx)

    def in_row(step):
        return (row, ((column + step) % columns) * 2 + core)

    def load(part, source, head):
        return pltpu.make_async_copy(
            source.at[:, head * HEAD_SIZE:(head + 1) * HEAD_SIZE],
            window.at[0, core, head, part],
            load_sem.at[part, head],
        )

    for head in range(KEY_VALUE_HEADS):
        load(0, k_hbm, head).start()
        load(1, v_hbm, head).start()
    load_q = pltpu.make_async_copy(q_hbm, q_ref, query_sem)
    load_q.start()

    barrier = pltpu.get_barrier_semaphore()
    partners = [in_row(step) for step in range(1, columns)]
    partners += [(next_row, ctx), (last_row, ctx), pair]
    partners += [relay_to, relayed_to, relayed_from]
    for partner in partners:
        pl.semaphore_signal(barrier, inc=1, device_id=partner, device_id_type=MESH)
    pl.semaphore_wait(barrier, len(partners))

    def along_rows(slot, head):
        return pltpu.make_async_remote_copy(
            src_ref=window.at[slot, core, head],
            dst_ref=window.at[slot + columns, core, head],
            send_sem=row_send_sem.at[slot, head],
            recv_sem=recv_sem.at[slot + columns, head],
            device_id=(next_row, ctx),
            device_id_type=MESH,
        )

    def to_relay(slot, head):
        return pltpu.make_async_remote_copy(
            src_ref=window.at[slot, core, head],
            dst_ref=relay.at[slot, head - DIRECT],
            send_sem=row_send_sem.at[slot, head],
            recv_sem=relay_recv_sem.at[slot, head - DIRECT],
            device_id=relay_to,
            device_id_type=MESH,
        )

    def from_relay(slot, head):
        return pltpu.make_async_remote_copy(
            src_ref=relay.at[slot, head - DIRECT],
            dst_ref=window.at[slot + columns, core, head],
            send_sem=relay_send_sem.at[slot, head - DIRECT],
            recv_sem=recv_sem.at[slot + columns, head],
            device_id=relayed_to,
            device_id_type=MESH,
        )

    def send_along_rows(slot, head):
        relayed = at_turn & (head >= DIRECT)

        @pl.when(relayed)
        def _():
            to_relay(slot, head).start()

        @pl.when(jnp.logical_not(relayed))
        def _():
            along_rows(slot, head).start()

    def pass_relayed(slot, head):
        @pl.when(at_turn & (head >= DIRECT))
        def _():
            piece = relay.at[slot, head - DIRECT]
            pltpu.make_async_copy(piece, piece, relay_recv_sem.at[slot, head - DIRECT]).wait()
            from_relay(slot, head).start()

    def along_columns(step, head):
        source = jnp.where(column + step < columns, 0, columns)
        return pltpu.make_async_remote_copy(
            src_ref=window.at[source, core, head],
            dst_ref=window.at[step, core, head],
            send_sem=column_send_sem.at[step, head],
            recv_sem=recv_sem.at[step, head],
            device_id=in_row(step),
            device_id_type=MESH,
        )

    def to_pair(slot, head):
        return pltpu.make_async_remote_copy(
            src_ref=window.at[slot, core, head],
            dst_ref=window.at[slot, core, head],
            send_sem=pair_send_sem.at[slot, head],
            recv_sem=pair_recv_sem.at[slot, head],
            device_id=pair,
            device_id_type=MESH,
        )

    def arrived(slot, head):
        piece = window.at[slot, core, head]
        pltpu.make_async_copy(piece, piece, recv_sem.at[slot, head]).wait()

    def pair_arrived(slot, head):
        piece = window.at[slot, 1 - core, head]
        pltpu.make_async_copy(piece, piece, pair_recv_sem.at[slot, head]).wait()

    for head in range(KEY_VALUE_HEADS):
        load(0, k_hbm, head).wait()
        load(1, v_hbm, head).wait()
        if head >= DIRECT:
            send_along_rows(0, head)
        else:
            along_rows(0, head).start()
        for step in (1, 3, 2):
            @pl.when(column + step < columns)
            def _():
                along_columns(step, head).start()
        to_pair(0, head).start()

    lengths = len_ref[...].astype(jnp.float32)
    ndocs = lengths.shape[1]
    sub = lax.broadcasted_iota(jnp.int32, (ndocs, ndocs), 0)
    lane = lax.broadcasted_iota(jnp.int32, (ndocs, ndocs), 1)
    as_column = jnp.sum(jnp.where(sub == lane, lengths, 0.0), axis=1, keepdims=True)
    ends = jnp.sum(jnp.where(sub <= lane, as_column, 0.0), axis=0, keepdims=True)
    begins = ends - lengths
    ends = ends.astype(jnp.int32)
    begins = begins.astype(jnp.int32)
    query_pos = (chip * 2 + core) * BLOCK + lax.broadcasted_iota(jnp.int32, (BLOCK, ndocs), 0)
    same = (query_pos >= begins) & (query_pos < ends)
    qmask_ref[...] = jnp.where(same, 0.0, NEG).astype(jnp.bfloat16)

    @pl.loop(0, SLOTS)
    def _(slot):
        key_pos = (chip - slot) * (2 * BLOCK) + lax.broadcasted_iota(
            jnp.int32, (2 * BLOCK, ndocs), 0
        )
        inside = ((key_pos >= begins) & (key_pos < ends)) | (key_pos < 0)
        hot_ref[slot] = jnp.where(inside, 1.0, 0.0).astype(jnp.bfloat16)

    load_q.wait()

    def attend(slots, head, first, last):
        count = 2 * BLOCK * len(slots)
        blocks = [(s, p) for s in slots for p in (0, 1)]
        key = jnp.concatenate([window[s, p, head, 0] for s, p in blocks], axis=0)
        hot = jnp.concatenate([hot_ref[s] for s in slots], axis=0)
        key = jnp.concatenate([key, hot], axis=1)
        value = jnp.concatenate([window[s, p, head, 1] for s, p in blocks], axis=0)
        value = jnp.concatenate([value, jnp.ones((count, HEAD_SIZE), jnp.bfloat16)], axis=1)
        for inner in range(0, GROUP, STACK):
            heads = [head * GROUP + inner + i for i in range(STACK)]
            spans = [
                pl.ds(pl.multiple_of(n * HEAD_SIZE, HEAD_SIZE), HEAD_SIZE) for n in heads
            ]
            query = jnp.concatenate([q_ref[:, span] for span in spans], axis=0)
            mask = jnp.concatenate([qmask_ref[...]] * STACK, axis=0)
            query = jnp.concatenate([query, mask], axis=1)
            scores = lax.dot_general(
                query, key, (((1,), (1,)), ((), ())), preferred_element_type=jnp.float32
            )
            rows = pl.ds(
                pl.multiple_of(heads[0] * BLOCK, STACK * BLOCK), STACK * BLOCK
            )
            if first:
                key_at = lax.broadcasted_iota(jnp.int32, scores.shape, 1)
                query_at = lax.broadcasted_iota(jnp.int32, scores.shape, 0) % BLOCK
                scores = jnp.where(key_at <= query_at + core * BLOCK, scores, NEG)
            top = jnp.max(scores, axis=1, keepdims=True)
            if first:
                top = jnp.broadcast_to(top, (STACK * BLOCK, HEAD_SIZE))
            else:
                old = max_ref[rows, :]
                top = jnp.maximum(old, top)
            wide = jnp.concatenate([top] * (count // HEAD_SIZE), axis=1)
            weights = jnp.exp2((scores - wide) * EXPONENT_SCALE).astype(jnp.bfloat16)
            total = jnp.dot(weights, value, preferred_element_type=jnp.float32)
            if not first:
                rescale = jnp.exp2((old - top) * EXPONENT_SCALE)
                total = acc_ref[rows, :] * jnp.concatenate([rescale] * 2, axis=1) + total
            if last:
                result = (total[:, :HEAD_SIZE] / total[:, HEAD_SIZE:]).astype(jnp.bfloat16)
                for i, span in enumerate(spans):
                    out_ref[:, span] = result[i * BLOCK:(i + 1) * BLOCK, :]
            else:
                acc_ref[rows, :] = total
                max_ref[rows, :] = top

    def own(head, carry):
        pair_arrived(0, head)
        attend([0], head, True, False)
        return carry

    def pass_on(head, carry):
        arrived(columns, head)
        for step in (1, 3, 2):
            @pl.when(column + step >= columns)
            def _():
                along_columns(step, head).start()
        send_along_rows(columns, head)
        to_pair(columns, head).start()
        pass_relayed(0, head)
        return carry

    def middle(head, carry):
        for slot in (1, 3, 2):
            arrived(slot, head)
            send_along_rows(slot, head)
            to_pair(slot, head).start()
        pass_relayed(columns, head)
        for slot in (1, 3, 2):
            pass_relayed(slot, head)
        arrived(8, head)
        to_pair(8, head).start()
        for pair_slots in ([4, 8], [1, 2]):
            for slot in pair_slots:
                pair_arrived(slot, head)
            attend(pair_slots, head, False, False)
        return carry

    def final(head, carry):
        for slot in (5, 7, 6):
            arrived(slot, head)
            to_pair(slot, head).start()
        for slot in (3, 5):
            pair_arrived(slot, head)
        attend([3, 5], head, False, False)
        for slot in (6, 7):
            pair_arrived(slot, head)
        attend([6, 7], head, False, True)
        return carry

    lax.fori_loop(0, KEY_VALUE_HEADS, own, 0)
    lax.fori_loop(0, KEY_VALUE_HEADS, pass_on, 0)
    lax.fori_loop(0, KEY_VALUE_HEADS, middle, 0)
    lax.fori_loop(0, KEY_VALUE_HEADS, final, 0)

    def drain(head, carry):
        for slot in range(columns + 1):
            along_rows(slot, head).wait_send()
        for step in range(1, columns):
            along_columns(step, head).wait_send()

        @pl.when(at_turn & (head >= DIRECT))
        def _():
            for slot in range(columns + 1):
                from_relay(slot, head).wait_send()

        for slot in range(SLOTS):
            to_pair(slot, head).wait_send()
        return carry

    lax.fori_loop(0, KEY_VALUE_HEADS, drain, 0)


def per_device(queries, keys, values, lengths):
    columns = lax.axis_size("ctx") // 2
    dp_size = lax.axis_size("dp")
    rows = queries.shape[0]
    ndocs = lengths.shape[0]
    any_space = pl.BlockSpec(memory_space=pl.ANY)
    vmem = pl.BlockSpec(memory_space=pltpu.VMEM)
    flops = 4 * rows * QUERY_HEADS * SLOTS * 2 * BLOCK * 2 * HEAD_SIZE
    return pl.pallas_call(
        functools.partial(kernel, dp_size, columns, TURN),
        out_shape=jax.ShapeDtypeStruct(queries.shape, jnp.bfloat16),
        in_specs=[any_space, any_space, any_space, vmem],
        out_specs=vmem,
        scratch_shapes=[
            pltpu.VMEM((SLOTS, 2, KEY_VALUE_HEADS, 2, BLOCK, HEAD_SIZE), jnp.bfloat16),
            pltpu.VMEM((columns + 1, RELAYED, 2, BLOCK, HEAD_SIZE), jnp.bfloat16),
            pltpu.VMEM(queries.shape, jnp.bfloat16),
            pltpu.VMEM((SLOTS, 2 * BLOCK, ndocs), jnp.bfloat16),
            pltpu.VMEM((BLOCK, ndocs), jnp.bfloat16),
            pltpu.VMEM((QUERY_HEADS * BLOCK, HEAD_SIZE), jnp.float32),
            pltpu.VMEM((QUERY_HEADS * BLOCK, 2 * HEAD_SIZE), jnp.float32),
            pltpu.SemaphoreType.DMA((2, KEY_VALUE_HEADS)),
            pltpu.SemaphoreType.DMA(()),
            pltpu.SemaphoreType.DMA((SLOTS, KEY_VALUE_HEADS)),
            pltpu.SemaphoreType.DMA((columns + 1, RELAYED)),
            pltpu.SemaphoreType.DMA((SLOTS, KEY_VALUE_HEADS)),
            pltpu.SemaphoreType.DMA((SLOTS, KEY_VALUE_HEADS)),
            pltpu.SemaphoreType.DMA((columns + 1, RELAYED)),
            pltpu.SemaphoreType.DMA((columns, KEY_VALUE_HEADS)),
            pltpu.SemaphoreType.DMA((SLOTS, KEY_VALUE_HEADS)),
        ],
        compiler_params=pltpu.CompilerParams(
            collective_id=0, has_side_effects=True, vmem_limit_bytes=48 * 1024 * 1024
        ),
        cost_estimate=pl.CostEstimate(
            flops=flops, bytes_accessed=4 * queries.size, transcendentals=0
        ),
    )(queries, keys, values, lengths.reshape(1, ndocs))


def solution(mesh):
    in_specs = (P(("dp", "ctx"), None), P(("dp", "ctx"), None), P(("dp", "ctx"), None), P())
    out_specs = P(("dp", "ctx"), None)
    return jax.shard_map(
        per_device, mesh=mesh, in_specs=in_specs, out_specs=out_specs, check_vma=False
    )
```

time: 95.9 us -> 82.1 us (0.86)
  Pallas kernels: 91.1 us -> 77.3 us
    pallas_call x1, Pallas kernels: 91.1 us -> 77.3 us  [per_device(): pl.pallas_call(functools.partial(kernel, dp_size, columns, TURN), out_sha...]
where the time goes in v1:
time: 82.1 us; the launch traced here: 81.9 us
  Pallas kernels  77.3 us (94%)
  local copies, waits for them, and re-layouts  4.66 us (6%)
    pallas_call x1, Pallas kernels, per_device(): pl.pallas_call(functools.partial(kernel, dp_size, columns, TURN), out_sha...  77.3 us
    unnamed x9, local copies, waits for them, and re-layouts  4.66 us

profile of v1, /device:TPU:1, one launch (start us, length us, event | category | flops | bytes accessed | tf_op | source)
XLA Modules:
  0.0 81.9 jit_solution(12953870414731156718)
XLA Ops:
  0.0 0.0 copy-start.3
  0.0 0.7 copy-done.3
  0.7 0.0 copy-start
  0.7 1.2 %copy-done = bf16[128,4096]{1,0:T(8,128)(2,1)S(1)} copy-done((bf16[128,4096]{1,0:T(8,128)(2,1)S(1)}, bf16[128,4096]{1,0:T(8,128)(2,1)}, u32[]{:S(2)}) %copy-start) | copy-done | bytes 1048600
  1.9 0.0 copy-start.1
  1.9 0.9 %copy-done.1 = bf16[128,512]{1,0:T(8,128)(2,1)S(1)} copy-done((bf16[128,512]{1,0:T(8,128)(2,1)S(1)}, bf16[128,512]{1,0:T(8,128)(2,1)}, u32[]{:S(2)}) %copy-start.1) | copy-done | bytes 131096
  2.8 0.0 copy-start.2
  2.8 0.9 %copy-done.2 = bf16[128,512]{1,0:T(8,128)(2,1)S(1)} copy-done((bf16[128,512]{1,0:T(8,128)(2,1)S(1)}, bf16[128,512]{1,0:T(8,128)(2,1)}, u32[]{:S(2)}) %copy-start.2) | copy-done | bytes 131096
  3.7 77.3 %shard_map.46 = bf16[128,4096]{1,0:T(8,128)(2,1)S(1)} custom-call(bf16[128,4096]{1,0:T(8,128)(2,1)S(1)} %copy-done, bf16[128,512]{1,0:T(8,128)(2,1)S(1)} %copy-done.1, bf16[128,512]{1,0:T(8,128)(2,1)S(1)} %copy-done.2, s32[1,128]{1,0:T(1,128)S(1)} %bitcast.1), custom_call_target="tpu_custom_call" | custom-call | flops 9663676416 | bytes 2097152 | tf_op jit(solution)/shard_map/pallas_call | solution.py:305
  81.0 1.0 %copy.6 = bf16[128,4096]{1,0:T(8,128)(2,1)} copy(bf16[128,4096]{1,0:T(8,128)(2,1)S(1)} %shard_map.46) | data formatting | bytes 2097152
Async XLA Ops:
  0.0 0.7 copy-start.3
  0.7 1.2 %copy-start = (bf16[128,4096]{1,0:T(8,128)(2,1)S(1)}, bf16[128,4096]{1,0:T(8,128)(2,1)}, u32[]{:S(2)}) copy-start(bf16[128,4096]{1,0:T(8,128)(2,1)} %q_hbm.1) | copy-start | bytes 3145732
  1.9 0.9 %copy-start.1 = (bf16[128,512]{1,0:T(8,128)(2,1)S(1)}, bf16[128,512]{1,0:T(8,128)(2,1)}, u32[]{:S(2)}) copy-start(bf16[128,512]{1,0:T(8,128)(2,1)} %k_hbm.1) | copy-start | bytes 393220
  2.8 0.9 %copy-start.2 = (bf16[128,512]{1,0:T(8,128)(2,1)S(1)}, bf16[128,512]{1,0:T(8,128)(2,1)}, u32[]{:S(2)}) copy-start(bf16[128,512]{1,0:T(8,128)(2,1)} %v_hbm.1) | copy-start | bytes 393220

commit v2 on v1

--- a/solution.py
+++ b/solution.py
@@ -15,6 +15,7 @@
 BLOCK = 128
 SLOTS = 9
 TURN = 8
+OLDER = (1, 3)
 RELAYED = 2
 STACK = 2
 DIRECT = KEY_VALUE_HEADS - RELAYED
@@ -27,7 +28,7 @@
     dp_size, columns, turn,
     q_hbm, k_hbm, v_hbm, len_ref, out_ref,
     window, relay, q_ref, hot_ref, qmask_ref, max_ref, acc_ref,
-    load_sem, query_sem, recv_sem, relay_recv_sem, pair_recv_sem, row_send_sem, relay_send_sem, column_send_sem, pair_send_sem,
+    load_sem, query_sem, recv_sem, relay_recv_sem, pair_recv_sem, row_send_sem, relay_send_sem, older_send_sem, column_send_sem, pair_send_sem,
 ):
     row = lax.axis_index("dp")
     ctx = lax.axis_index("ctx")
@@ -40,6 +41,7 @@
         return of_row + turn - 2 * turn * (of_row // turn % 2)
 
     at_turn = row % turn == turn - 1
+    after_turn = row % turn == 0
     relay_to = (beside(row), ctx)
     relayed_to = ((beside(row) + 1) % dp_size, ctx)
     relayed_from = (beside(last_row), ctx)
@@ -127,6 +129,17 @@
             device_id_type=MESH,
         )
 
+    def older_along_columns(step, head):
+        source = jnp.where(column + step < columns, columns, 2 * columns)
+        return pltpu.make_async_remote_copy(
+            src_ref=window.at[source, core, head],
+            dst_ref=window.at[step + columns, core, head],
+            send_sem=older_send_sem.at[step, head],
+            recv_sem=recv_sem.at[step + columns, head],
+            device_id=in_row(step),
+            device_id_type=MESH,
+        )
+
     def to_pair(slot, head):
         return pltpu.make_async_remote_copy(
             src_ref=window.at[slot, core, head],
@@ -152,7 +165,7 @@
             send_along_rows(0, head)
         else:
             along_rows(0, head).start()
-        for step in (1, 3, 2):
+        for step in (2, 1, 3):
             @pl.when(column + step < columns)
             def _():
                 along_columns(step, head).start()
@@ -227,33 +240,47 @@
                 acc_ref[rows, :] = total
                 max_ref[rows, :] = top
 
-    def own(head, carry):
-        pair_arrived(0, head)
-        attend([0], head, True, False)
-        return carry
-
     def pass_on(head, carry):
         arrived(columns, head)
-        for step in (1, 3, 2):
+        for step in (2, 1, 3):
             @pl.when(column + step >= columns)
             def _():
                 along_columns(step, head).start()
+        for step in OLDER:
+            @pl.when(after_turn & (column + step < columns))
+            def _():
+                older_along_columns(step, head).start()
         send_along_rows(columns, head)
         to_pair(columns, head).start()
         pass_relayed(0, head)
+        pair_arrived(0, head)
+        attend([0], head, True, False)
+        return carry
+
+    def pass_oldest(head, carry):
+        pass_relayed(columns, head)
+        arrived(2 * columns, head)
+        for step in OLDER:
+            @pl.when(after_turn & (column + step >= columns))
+            def _():
+                older_along_columns(step, head).start()
+        to_pair(2 * columns, head).start()
         return carry
 
     def middle(head, carry):
+        for slot in (2, 1, 3):
+            arrived(slot, head)
+            if slot in OLDER:
+                @pl.when(jnp.logical_not(at_turn))
+                def _():
+                    along_rows(slot, head).start()
+            else:
+                send_along_rows(slot, head)
+            to_pair(slot, head).start()
         for slot in (1, 3, 2):
-            arrived(slot, head)
-            send_along_rows(slot, head)
-            to_pair(slot, head).start()
-        pass_relayed(columns, head)
-        for slot in (1, 3, 2):
-            pass_relayed(slot, head)
-        arrived(8, head)
-        to_pair(8, head).start()
-        for pair_slots in ([4, 8], [1, 2]):
+            if slot not in OLDER:
+                pass_relayed(slot, head)
+        for pair_slots in ([4, 8], [1, 2, 3]):
             for slot in pair_slots:
                 pair_arrived(slot, head)
             attend(pair_slots, head, False, False)
@@ -263,29 +290,36 @@
         for slot in (5, 7, 6):
             arrived(slot, head)
             to_pair(slot, head).start()
-        for slot in (3, 5):
+        for slot in (5, 6, 7):
             pair_arrived(slot, head)
-        attend([3, 5], head, False, False)
-        for slot in (6, 7):
-            pair_arrived(slot, head)
-        attend([6, 7], head, False, True)
-        return carry
-
-    lax.fori_loop(0, KEY_VALUE_HEADS, own, 0)
+        attend([5, 6, 7], head, False, True)
+        return carry
+
     lax.fori_loop(0, KEY_VALUE_HEADS, pass_on, 0)
+    lax.fori_loop(0, KEY_VALUE_HEADS, pass_oldest, 0)
     lax.fori_loop(0, KEY_VALUE_HEADS, middle, 0)
     lax.fori_loop(0, KEY_VALUE_HEADS, final, 0)
 
     def drain(head, carry):
         for slot in range(columns + 1):
-            along_rows(slot, head).wait_send()
+            if slot not in OLDER:
+                along_rows(slot, head).wait_send()
+        for step in OLDER:
+            @pl.when(jnp.logical_not(at_turn))
+            def _():
+                along_rows(step, head).wait_send()
+
+            @pl.when(after_turn)
+            def _():
+                older_along_columns(step, head).wait_send()
         for step in range(1, columns):
             along_columns(step, head).wait_send()
 
         @pl.when(at_turn & (head >= DIRECT))
         def _():
             for slot in range(columns + 1):
-                from_relay(slot, head).wait_send()
+                if slot not in OLDER:
+                    from_relay(slot, head).wait_send()
 
         for slot in range(SLOTS):
             to_pair(slot, head).wait_send()
@@ -323,6 +357,7 @@
             pltpu.SemaphoreType.DMA((SLOTS, KEY_VALUE_HEADS)),
             pltpu.SemaphoreType.DMA((columns + 1, RELAYED)),
             pltpu.SemaphoreType.DMA((columns, KEY_VALUE_HEADS)),
+            pltpu.SemaphoreType.DMA((columns, KEY_VALUE_HEADS)),
             pltpu.SemaphoreType.DMA((SLOTS, KEY_VALUE_HEADS)),
         ],
         compiler_params=pltpu.CompilerParams(

time: 82.1 us -> 77.4 us (0.943)
  Pallas kernels: 77.3 us -> 72.6 us
    pallas_call x1, Pallas kernels: 77.3 us -> 72.6 us  [per_device(): pl.pallas_call(functools.partial(kernel, dp_size, columns, TURN), out_sha...]
where the time goes in v2:
time: 77.4 us; the launch traced here: 77.3 us
  Pallas kernels  72.6 us (94%)
  local copies, waits for them, and re-layouts  4.66 us (6%)
    pallas_call x1, Pallas kernels, per_device(): pl.pallas_call(functools.partial(kernel, dp_size, columns, TURN), out_sha...  72.6 us
    unnamed x9, local copies, waits for them, and re-layouts  4.66 us

profile of v2, /device:TPU:1, one launch (start us, length us, event | category | flops | bytes accessed | tf_op | source)
XLA Modules:
  0.0 77.3 jit_solution(15397367926768788110)
XLA Ops:
  0.0 0.0 copy-start.3
  0.0 0.7 copy-done.3
  0.7 0.0 copy-start
  0.7 1.2 %copy-done = bf16[128,4096]{1,0:T(8,128)(2,1)S(1)} copy-done((bf16[128,4096]{1,0:T(8,128)(2,1)S(1)}, bf16[128,4096]{1,0:T(8,128)(2,1)}, u32[]{:S(2)}) %copy-start) | copy-done | bytes 1048600
  1.9 0.0 copy-start.1
  1.9 0.9 %copy-done.1 = bf16[128,512]{1,0:T(8,128)(2,1)S(1)} copy-done((bf16[128,512]{1,0:T(8,128)(2,1)S(1)}, bf16[128,512]{1,0:T(8,128)(2,1)}, u32[]{:S(2)}) %copy-start.1) | copy-done | bytes 131096
  2.8 0.0 copy-start.2
  2.8 0.9 %copy-done.2 = bf16[128,512]{1,0:T(8,128)(2,1)S(1)} copy-done((bf16[128,512]{1,0:T(8,128)(2,1)S(1)}, bf16[128,512]{1,0:T(8,128)(2,1)}, u32[]{:S(2)}) %copy-start.2) | copy-done | bytes 131096
  3.7 72.6 %shard_map.46 = bf16[128,4096]{1,0:T(8,128)(2,1)S(1)} custom-call(bf16[128,4096]{1,0:T(8,128)(2,1)S(1)} %copy-done, bf16[128,512]{1,0:T(8,128)(2,1)S(1)} %copy-done.1, bf16[128,512]{1,0:T(8,128)(2,1)S(1)} %copy-done.2, s32[1,128]{1,0:T(1,128)S(1)} %bitcast.1), custom_call_target="tpu_custom_call" | custom-call | flops 9663676416 | bytes 2097152 | tf_op jit(solution)/shard_map/pallas_call | solution.py:339
  76.3 1.0 %copy.6 = bf16[128,4096]{1,0:T(8,128)(2,1)} copy(bf16[128,4096]{1,0:T(8,128)(2,1)S(1)} %shard_map.46) | data formatting | bytes 2097152
Async XLA Ops:
  0.0 0.7 copy-start.3
  0.7 1.2 %copy-start = (bf16[128,4096]{1,0:T(8,128)(2,1)S(1)}, bf16[128,4096]{1,0:T(8,128)(2,1)}, u32[]{:S(2)}) copy-start(bf16[128,4096]{1,0:T(8,128)(2,1)} %q_hbm.1) | copy-start | bytes 3145732
  1.9 0.9 %copy-start.1 = (bf16[128,512]{1,0:T(8,128)(2,1)S(1)}, bf16[128,512]{1,0:T(8,128)(2,1)}, u32[]{:S(2)}) copy-start(bf16[128,512]{1,0:T(8,128)(2,1)} %k_hbm.1) | copy-start | bytes 393220
  2.8 0.9 %copy-start.2 = (bf16[128,512]{1,0:T(8,128)(2,1)S(1)}, bf16[128,512]{1,0:T(8,128)(2,1)}, u32[]{:S(2)}) copy-start(bf16[128,512]{1,0:T(8,128)(2,1)} %v_hbm.1) | copy-start | bytes 393220
